TPU v7x, 128 devices: a whole 4x4x4 slice. The times are simulated.
128 devices in a mesh: gx: 8 (over z, x_lo), gy: 4 (over x_hi, core), ha: 4 (over y).
Axes of the slice: x: 4 (x_hi: 2, x_lo: 2; x = x_hi * 2 + x_lo), y: 4, z: 4, core: 2. Of those that a mesh axis runs over, the one named last changes fastest.
Arguments:
- tokens: bfloat16 [64, 64, 16, 384], P('gx', 'gy'), may hold values from -30 to 30
- input_weight: bfloat16 [384, 768], P(None, 'ha'), may hold values from -1 to 1
- output_weight: bfloat16 [256, 384], P('ha'), may hold values from -0.375 to 0.375
- tissue_bits: int32 [64, 64], P('gx', 'gy'), may hold values from 0 to 65535
- cotangent: bfloat16 [64, 64, 16, 384], P('gx', 'gy'), may hold values from -6 to 6
Outputs:
- token_gradient: bfloat16 [64, 64, 16, 384], P('gx', 'gy', None, 'ha')
- input_gradient: float32 [384, 768], P(None, 'ha')
- output_gradient: float32 [256, 384], P('ha')
All inputs are finite; a program needn't handle non-finite values.
Results may differ from a plain program's by a relative error of at most 0.018.
The roundings to bfloat16 on the way count: a program that leaves them out, or rounds other values in their place, can miss the bound.
Values may be sent and summed in bfloat16 or wider, within the bound.
No kernel may reach another device: no remote copies, remote signals or barrier semaphores. Data moves between devices by JAX's collectives and lax.ppermute only.
A program may use at most 128 MiB of HBM per device.

v0:
```python
import jax
import jax.numpy as jnp
from jax import lax
from jax.sharding import PartitionSpec as P

HD = 64
REACH = 3


def extended(block, sides, width):
    for axis, dim in sides:
        count = lax.axis_size(axis)
        forward = [(i, i + 1) for i in range(count - 1)]
        backward = [(target, source) for source, target in forward]
        low = lax.ppermute(
            lax.slice_in_dim(block, block.shape[dim] - width, None, axis=dim), axis, forward
        )
        high = lax.ppermute(lax.slice_in_dim(block, 0, width, axis=dim), axis, backward)
        block = jnp.concatenate([low, block, high], axis=dim)
    return block


def block_length(extent, plane_rows):
    for length in range(1, extent + 1):
        if extent % length == 0 and length * plane_rows >= 512:
            return length
    return extent


def shards(tokens, input_weight, output_weight, tissue_bits, cotangent):
    width_x, width_y, depth, model_width = tokens.shape
    local_heads = output_weight.shape[0] // HD
    token_count = width_x * width_y * depth
    score_scale = HD ** (-0.5)
    flat_tokens = tokens.reshape(token_count, model_width)
    flat_cotangent = cotangent.reshape(token_count, model_width)
    bit_values = 2 ** jnp.arange(depth, dtype=jnp.int32)
    key_valid = (tissue_bits[:, :, None] // bit_values % 2).astype(jnp.bfloat16)
    key_span_x_full = width_x + 2 * REACH
    key_span_y = width_y + 2 * REACH
    projected = jnp.dot(flat_tokens, input_weight, preferred_element_type=jnp.float32).astype(
        jnp.bfloat16
    )
    projected = projected.reshape(token_count, local_heads, 3, HD)
    queries = projected[:, :, 0, :].reshape(token_count, local_heads * HD)
    pair_local = projected[:, :, 1:, :].reshape(width_x, width_y, depth, local_heads * 2 * HD)
    pair_padded, valid_padded = (
        extended(pair_local, (("gx", 0), ("gy", 1)), REACH),
        extended(key_valid, (("gx", 0), ("gy", 1)), REACH),
    )
    upstream = jnp.einsum(
        "nd,ed->ne", flat_cotangent, output_weight, preferred_element_type=jnp.float32
    ).astype(jnp.bfloat16)
    block_x = block_length(width_x, width_y * depth)
    block_count = width_x // block_x
    key_span_x = block_x + 2 * REACH
    query_rows = block_x * width_y * depth
    key_rows = key_span_x * key_span_y * depth
    query_slots = jnp.arange(query_rows)
    query_x = query_slots // (width_y * depth)
    query_y = query_slots // depth % width_y
    query_z = query_slots % depth
    key_slots = jnp.arange(key_rows)
    key_x = key_slots // (key_span_y * depth) - REACH
    key_y = key_slots // depth % key_span_y - REACH
    key_z = key_slots % depth
    within = (
        (jnp.abs(query_x[:, None] - key_x[None, :]) <= REACH)
        & (jnp.abs(query_y[:, None] - key_y[None, :]) <= REACH)
        & (jnp.abs(query_z[:, None] - key_z[None, :]) <= REACH)
    )
    self_pair = (
        (query_x[:, None] == key_x[None, :])
        & (query_y[:, None] == key_y[None, :])
        & (query_z[:, None] == key_z[None, :])
    )
    query_grid = queries.reshape(width_x, width_y, depth, local_heads, HD)
    upstream_grid = upstream.reshape(width_x, width_y, depth, local_heads, HD)
    pair_grid = pair_padded.reshape(key_span_x_full, key_span_y, depth, local_heads, 2, HD)

    def attend_block(block_index, carry):
        query_sums, pair_sums, outputs = carry
        first_row = block_index * block_x
        query_block = lax.dynamic_slice_in_dim(query_grid, first_row, block_x, 0).reshape(
            query_rows, local_heads, HD
        )
        upstream_block = lax.dynamic_slice_in_dim(upstream_grid, first_row, block_x, 0).reshape(
            query_rows, local_heads, HD
        )
        pair_block = lax.dynamic_slice_in_dim(pair_grid, first_row, key_span_x, 0).reshape(
            key_rows, local_heads, 2, HD
        )
        keys_block = pair_block[:, :, 0, :]
        values_block = pair_block[:, :, 1, :]
        live_keys = (
            lax.dynamic_slice_in_dim(valid_padded, first_row, key_span_x, 0).reshape(key_rows) > 0
        )
        allowed = within & (live_keys[None, :] | self_pair)
        scores = (
            jnp.einsum("qhe,khe->hqk", query_block, keys_block, preferred_element_type=jnp.float32)
            * score_scale
        )
        scores = jnp.where(allowed[None], scores, -jnp.inf)
        row_max = jnp.max(scores, axis=-1, keepdims=True)
        raised = jnp.exp(scores - row_max)
        weights = (raised / jnp.sum(raised, axis=-1, keepdims=True)).astype(jnp.bfloat16)
        result = jnp.einsum(
            "hqk,khe->qhe", weights, values_block, preferred_element_type=jnp.float32
        )
        weight_gradient = jnp.einsum(
            "qhe,khe->hqk", upstream_block, values_block, preferred_element_type=jnp.float32
        )
        row_inner = jnp.sum(upstream_block.astype(jnp.float32) * result, axis=-1)
        score_gradient = (
            weights.astype(jnp.float32) * (weight_gradient - row_inner.T[:, :, None]) * score_scale
        ).astype(jnp.bfloat16)
        query_gradient = jnp.einsum(
            "hqk,khe->qhe", score_gradient, keys_block, preferred_element_type=jnp.float32
        )
        key_gradient = jnp.einsum(
            "hqk,qhe->khe", score_gradient, query_block, preferred_element_type=jnp.float32
        )
        value_gradient = jnp.einsum(
            "hqk,qhe->khe", weights, upstream_block, preferred_element_type=jnp.float32
        )
        pair_gradient = jnp.stack([key_gradient, value_gradient], axis=2).reshape(
            key_span_x, key_span_y, depth, local_heads * 2 * HD
        )
        query_sums = lax.dynamic_update_slice_in_dim(
            query_sums,
            query_gradient.reshape(block_x, width_y, depth, local_heads * HD),
            first_row,
            0,
        )
        previous = lax.dynamic_slice_in_dim(pair_sums, first_row, key_span_x, 0)
        pair_sums = lax.dynamic_update_slice_in_dim(
            pair_sums, previous + pair_gradient, first_row, 0
        )
        outputs = lax.dynamic_update_slice_in_dim(
            outputs,
            result.astype(jnp.bfloat16).reshape(block_x, width_y, depth, local_heads * HD),
            first_row,
            0,
        )
        return (query_sums, pair_sums, outputs)

    start = (
        jnp.zeros((width_x, width_y, depth, local_heads * HD), jnp.float32),
        jnp.zeros((key_span_x_full, key_span_y, depth, local_heads * 2 * HD), jnp.float32),
        jnp.zeros((width_x, width_y, depth, local_heads * HD), jnp.bfloat16),
    )
    query_sums, pair_sums, outputs = lax.fori_loop(0, block_count, attend_block, start)
    rims_first = jnp.concatenate([pair_sums[:REACH], pair_sums[width_x + REACH :]], axis=0)
    from_first = extended(rims_first.astype(jnp.bfloat16), (("gx", 0),), REACH).astype(
        rims_first.dtype
    )
    interior = pair_sums[REACH : width_x + REACH]
    interior = interior.at[:REACH].add(from_first[:REACH])
    interior = interior.at[width_x - REACH :].add(from_first[3 * REACH :])
    rims_second = jnp.concatenate([interior[:, :REACH], interior[:, width_y + REACH :]], axis=1)
    from_second = extended(rims_second.astype(jnp.bfloat16), (("gy", 1),), REACH).astype(
        rims_second.dtype
    )
    centre = interior[:, REACH : width_y + REACH]
    centre = centre.at[:, :REACH].add(from_second[:, :REACH])
    centre = centre.at[:, width_y - REACH :].add(from_second[:, 3 * REACH :])
    query_part = query_sums.reshape(token_count, local_heads, 1, HD)
    pair_part = centre.reshape(token_count, local_heads, 2, HD)
    dprojected = (
        jnp.concatenate([query_part, pair_part], axis=2)
        .reshape(token_count, local_heads * 3 * HD)
        .astype(jnp.bfloat16)
    )
    partial_terms = jnp.einsum(
        "nc,dc->nd", dprojected, input_weight, preferred_element_type=jnp.float32
    ).reshape(width_x, width_y, depth, model_width)
    token_gradient = lax.psum_scatter(partial_terms, "ha", scatter_dimension=3, tiled=True).astype(
        jnp.bfloat16
    )
    attended_flat = outputs.reshape(token_count, local_heads * HD)
    part_input = jnp.einsum(
        "nd,nc->dc", flat_tokens, dprojected, preferred_element_type=jnp.float32
    )
    part_output = jnp.einsum(
        "ne,nd->ed", attended_flat, flat_cotangent, preferred_element_type=jnp.float32
    )
    summed_input, summed_output = (
        lax.psum(part_input.astype(jnp.bfloat16), ("gx", "gy")).astype(jnp.float32),
        lax.psum(part_output.astype(jnp.bfloat16), ("gx", "gy")).astype(jnp.float32),
    )
    normaliser = (token_count * lax.axis_size("gx") * lax.axis_size("gy")) ** (-0.5)
    return (token_gradient, summed_input * normaliser, summed_output * normaliser)


def solution(mesh):
    placed = (
        P("gx", "gy", None, None),
        P(None, "ha"),
        P("ha", None),
        P("gx", "gy"),
        P("gx", "gy", None, None),
    )
    return jax.shard_map(
        shards,
        mesh=mesh,
        in_specs=placed,
        out_specs=(P("gx", "gy", None, "ha"), P(None, "ha"), P("ha", None)),
        check_vma=False,
    )
```

profile of v0, /device:TPU:0, one launch (start us, length us, event | category | flops | bytes accessed | tf_op | source)
XLA Modules:
  0.0 429.6 jit_solution(15858001204018962524)
XLA Ops:
  11.0 3.5 collective-permute-start.4
  24.8 5.9 %collective-permute-start = (bf16[3,16,16,128]{3,2,1,0:T(8,128)(2,1)}, bf16[3,16,16,128]{3,2,1,0:T(8,128)(2,1)}, u32[]{:S(2)}, u32[]{:S(2)}) collective-permute-start(bf16[3,16,16,128]{3,2,1,0:T(8,128)(2,1)} %slice.209), channel_id=1, source_target_pairs={{0,16},{16,32},{32,48},{48,64},{64,80},{80,96},{96,112},{1,17},{17... | collective-permute-start | bytes 589832 | tf_op jit(solution)/shard_map/ppermute | solution.py:15
  41.4 6.2 %collective-permute-start.2 = (bf16[14,3,16,128]{3,2,1,0:T(8,128)(2,1)S(1)}, bf16[14,3,16,128]{3,2,1,0:T(8,128)(2,1)S(1)}, u32[]{:S(2)}, u32[]{:S(2)}) collective-permute-start(bf16[14,3,16,128]{3,2,1,0:T(8,128)(2,1)S(1)} %get-tuple-element.401), channel_id=1, source_target_pairs={{0,4},{4,8},{8,12},{1,5},{5,9},{9,13},{2,6},{6,10},{10,14},{3,7},{... | collective-permute-start | bytes 516104 | tf_op jit(solution)/shard_map/ppermute | solution.py:15
  60.7 128.2 %while.23 = (s32[]{:T(128)}, bf16[8,16,16,64]{3,2,1,0:T(8,128)(2,1)}, f32[14,22,16,128]{3,2,1,0:T(8,128)}, bf16[8,16,16,64]{3,2,1,0:T(8,128)(2,1)}, bf16[14,22,1...) while((s32[]{:T(128)}, ...), condition=%wide.region_4.5_spmd.clone.clone, body=%wide.region_0.4_spmd.clone.clone.sunk | while | flops 1152845056 | bytes 82846784 | solution.py:152
  66.3 5.8 %fusion.85 = (f32[512]{0:T(512)S(1)}, f32[512,2816]{1,0:T(8,128)S(1)}) fusion(bf16[512,64]{1,0:T(8,128)(2,1)S(1)} %bitcast.150, bf16[2816,1,2,64]{3,0,2,1:T(8,128)(2,1)S(1)} %bitcast.143, pred[2816]{0:T(1024)(128)(4,1)S(1)} %gt.22, s32[2816]{0:T(1024)S(1)} %get-tuple-element.564, s32[512]{0:T(512)S(1)} %get-tuple-element.565, ...), kind=kOutput, calls=%fused_computation.123.clone.1 | convolution fusion | flops 214826496 | bytes 6667264 | tf_op jit(solution)/shard_map/while/body/eval_jaxpr/qhe,khe->hqk/dot_general | solution.py:100
  83.6 3.3 copy.74
  86.9 3.2 reshape.514
  98.4 5.8 %fusion.85 = (f32[512]{0:T(512)S(1)}, f32[512,2816]{1,0:T(8,128)S(1)}) fusion(bf16[512,64]{1,0:T(8,128)(2,1)S(1)} %bitcast.150, bf16[2816,1,2,64]{3,0,2,1:T(8,128)(2,1)S(1)} %bitcast.143, pred[2816]{0:T(1024)(128)(4,1)S(1)} %gt.22, s32[2816]{0:T(1024)S(1)} %get-tuple-element.564, s32[512]{0:T(512)S(1)} %get-tuple-element.565, ...), kind=kOutput, calls=%fused_computation.123.clone.1 | convolution fusion | flops 214826496 | bytes 6667264 | tf_op jit(solution)/shard_map/while/body/eval_jaxpr/qhe,khe->hqk/dot_general | solution.py:100
  115.7 3.3 copy.74
  119.0 3.2 reshape.514
  130.4 5.8 %fusion.85 = (f32[512]{0:T(512)S(1)}, f32[512,2816]{1,0:T(8,128)S(1)}) fusion(bf16[512,64]{1,0:T(8,128)(2,1)S(1)} %bitcast.150, bf16[2816,1,2,64]{3,0,2,1:T(8,128)(2,1)S(1)} %bitcast.143, pred[2816]{0:T(1024)(128)(4,1)S(1)} %gt.22, s32[2816]{0:T(1024)S(1)} %get-tuple-element.564, s32[512]{0:T(512)S(1)} %get-tuple-element.565, ...), kind=kOutput, calls=%fused_computation.123.clone.1 | convolution fusion | flops 214826496 | bytes 6667264 | tf_op jit(solution)/shard_map/while/body/eval_jaxpr/qhe,khe->hqk/dot_general | solution.py:100
  147.8 3.3 copy.74
  151.0 3.2 reshape.514
  162.5 5.8 %fusion.85 = (f32[512]{0:T(512)S(1)}, f32[512,2816]{1,0:T(8,128)S(1)}) fusion(bf16[512,64]{1,0:T(8,128)(2,1)S(1)} %bitcast.150, bf16[2816,1,2,64]{3,0,2,1:T(8,128)(2,1)S(1)} %bitcast.143, pred[2816]{0:T(1024)(128)(4,1)S(1)} %gt.22, s32[2816]{0:T(1024)S(1)} %get-tuple-element.564, s32[512]{0:T(512)S(1)} %get-tuple-element.565, ...), kind=kOutput, calls=%fused_computation.123.clone.1 | convolution fusion | flops 214826496 | bytes 6667264 | tf_op jit(solution)/shard_map/while/body/eval_jaxpr/qhe,khe->hqk/dot_general | solution.py:100
  179.8 3.3 copy.74
  191.0 3.6 collective-permute-start.8
  198.5 7.3 %collective-permute-done.9 = bf16[3,22,16,128]{3,2,1,0:T(8,128)(2,1)S(1)} collective-permute-done((bf16[3,22,16,128]{3,2,1,0:T(8,128)(2,1)S(1)}, bf16[3,22,16,128]{3,2,1,0:T(8,128)(2,1)S(1)}, u32[]{:S(2)}, u32[]{:S(2)}) %collective-permute-start.9) | collective-permute-done | bytes 270368 | tf_op jit(solution)/shard_map/ppermute | solution.py:18
  206.8 6.8 %collective-permute-start.10 = (bf16[8,3,16,128]{3,2,1,0:T(8,128)(2,1)}, bf16[8,3,16,128]{3,2,1,0:T(8,128)(2,1)}, u32[]{:S(2)}, u32[]{:S(2)}) collective-permute-start(bf16[8,3,16,128]{3,2,1,0:T(8,128)(2,1)} %get-tuple-element.405), channel_id=1, source_target_pairs={{0,4},{4,8},{8,12},{1,5},{5,9},{9,13},{2,6},{6,10},{10,14},{3,7},{... | collective-permute-start | bytes 294920 | tf_op jit(solution)/shard_map/ppermute | solution.py:15
  230.4 4.1 convert_element_type.112
  236.9 20.4 %copy.58 = f32[8,16,16,384]{2,1,0,3:T(8,128)} copy(f32[8,16,16,384]{3,2,1,0:T(8,128)} %fusion.14) | data formatting | bytes 6291456
  257.2 21.8 %reshape.511 = f32[384,2048]{1,0:T(8,128)} reshape(f32[384,8,16,16]{3,2,1,0:T(8,128)} %bitcast.147) | data formatting | bytes 6291456
  281.9 128.5 %psum.15 = bf16[64,384]{1,0:T(8,128)(2,1)S(1)} all-reduce(bf16[64,384]{1,0:T(8,128)(2,1)S(1)} %fusion.9), channel_id=1, replica_groups=mesh['gx'=8,'gy'=4,'ha'=4] {'gx','gy'}, use_global_device_ids=true, to_apply=%region_7.8 | all-reduce | flops 24576 | bytes 98304 | tf_op jit(solution)/shard_map/psum | solution.py:189
  412.7 4.7 %reshape.512 = bf16[96,8,16,16]{3,2,1,0:T(8,128)(2,1)} reshape(f32[96,2048]{1,0:T(8,128)} %reduce-scatter.4.cloned.1.call-done) | data formatting | bytes 1179648
  417.4 4.8 %copy.59 = bf16[8,16,16,96]{3,2,1,0:T(8,128)(2,1)} copy(bf16[8,16,16,96]{2,1,0,3:T(8,128)(2,1)} %bitcast.154) | data formatting | bytes 786432
  (197 shorter events, 150.0 us)
Async XLA Ops:
  8.0 7.8 %copy-start = (bf16[8,16,16,384]{3,2,1,0:T(8,128)(2,1)S(1)}, bf16[8,16,16,384]{3,2,1,0:T(8,128)(2,1)}, u32[]{:S(2)}) copy-start(bf16[8,16,16,384]{3,2,1,0:T(8,128)(2,1)} %param.15) | copy-start | bytes 4718596
  8.0 403.1 %all-reduce.2.cloned.1.call-start = ((), (), s32[]{:S(2)}) async-start(), calls=%async_computation.1 | async-start | bytes 294912 | tf_op jit(solution)/shard_map/psum | solution.py:188
  10.3 5.4 %copy-start.11 = (bf16[8,16,16]{2,1,0:T(8,128)(2,1)}, bf16[8,16,16]{2,1,0:T(8,128)(2,1)S(1)}, u32[]{:S(2)}) copy-start(bf16[8,16,16]{2,1,0:T(8,128)(2,1)S(1)} %fusion.17) | copy-start | bytes 12292
  11.0 24.1 %collective-permute-start.4 = (bf16[3,16,16]{2,1,0:T(8,128)(2,1)}, bf16[3,16,16]{2,1,0:T(8,128)(2,1)S(1)}, u32[]{:S(2)}, u32[]{:S(2)}) collective-permute-start(bf16[3,16,16]{2,1,0:T(8,128)(2,1)} %get-tuple-element.409), channel_id=1, source_target_pairs={{0,16},{16,32},{32,48},{48,64},{64,80},{80,96},{96,112},{1,17},{17... | collective-permute-start | bytes 4616 | tf_op jit(solution)/shard_map/ppermute | solution.py:15
  14.5 20.6 %collective-permute-start.5 = (bf16[3,16,16]{2,1,0:T(8,128)(2,1)}, bf16[3,16,16]{2,1,0:T(8,128)(2,1)}, u32[]{:S(2)}, u32[]{:S(2)}) collective-permute-start(bf16[3,16,16]{2,1,0:T(8,128)(2,1)} %get-tuple-element.410), channel_id=1, source_target_pairs={{16,0},{32,16},{48,32},{64,48},{80,64},{96,80},{112,96},{17,1},{33... | collective-permute-start | bytes 4616 | tf_op jit(solution)/shard_map/ppermute | solution.py:18
  15.8 15.5 %copy-start.4 = (bf16[8,16,16,384]{3,2,1,0:T(8,128)(2,1)S(1)}, bf16[8,16,16,384]{3,2,1,0:T(8,128)(2,1)}, u32[]{:S(2)}) copy-start(bf16[8,16,16,384]{3,2,1,0:T(8,128)(2,1)} %param.19) | copy-start | bytes 4718596
  21.4 18.1 %collective-permute-start.1 = (bf16[3,16,16,128]{3,2,1,0:T(8,128)(2,1)}, bf16[3,16,16,128]{3,2,1,0:T(8,128)(2,1)}, u32[]{:S(2)}, u32[]{:S(2)}) collective-permute-start(bf16[3,16,16,128]{3,2,1,0:T(8,128)(2,1)} %slice.212), channel_id=1, source_target_pairs={{16,0},{32,16},{48,32},{64,48},{80,64},{96,80},{112,96},{17,1},{33... | collective-permute-start | bytes 589832 | tf_op jit(solution)/shard_map/ppermute | solution.py:18
  24.8 13.6 %collective-permute-start = (bf16[3,16,16,128]{3,2,1,0:T(8,128)(2,1)}, bf16[3,16,16,128]{3,2,1,0:T(8,128)(2,1)}, u32[]{:S(2)}, u32[]{:S(2)}) collective-permute-start(bf16[3,16,16,128]{3,2,1,0:T(8,128)(2,1)} %slice.209), channel_id=1, source_target_pairs={{0,16},{16,32},{32,48},{48,64},{64,80},{80,96},{96,112},{1,17},{17... | collective-permute-start | bytes 589832 | tf_op jit(solution)/shard_map/ppermute | solution.py:15
  35.8 16.2 %collective-permute-start.6 = (bf16[14,3,16]{2,1,0:T(4,128)(2,1)S(1)}, bf16[14,3,16]{2,1,0:T(4,128)(2,1)S(1)}, u32[]{:S(2)}, u32[]{:S(2)}) collective-permute-start(bf16[14,3,16]{2,1,0:T(4,128)(2,1)S(1)} %get-tuple-element.407), channel_id=1, source_target_pairs={{0,4},{4,8},{8,12},{1,5},{5,9},{9,13},{2,6},{6,10},{10,14},{3,7},{... | collective-permute-start | bytes 4040 | tf_op jit(solution)/shard_map/ppermute | solution.py:15
  37.1 14.9 %collective-permute-start.7 = (bf16[14,3,16]{2,1,0:T(4,128)(2,1)S(1)}, bf16[14,3,16]{2,1,0:T(4,128)(2,1)S(1)}, u32[]{:S(2)}, u32[]{:S(2)}) collective-permute-start(bf16[14,3,16]{2,1,0:T(4,128)(2,1)S(1)} %get-tuple-element.408), channel_id=1, source_target_pairs={{4,0},{8,4},{12,8},{5,1},{9,5},{13,9},{6,2},{10,6},{14,10},{7,3},{... | collective-permute-start | bytes 4040 | tf_op jit(solution)/shard_map/ppermute | solution.py:18
  41.4 12.0 %collective-permute-start.2 = (bf16[14,3,16,128]{3,2,1,0:T(8,128)(2,1)S(1)}, bf16[14,3,16,128]{3,2,1,0:T(8,128)(2,1)S(1)}, u32[]{:S(2)}, u32[]{:S(2)}) collective-permute-start(bf16[14,3,16,128]{3,2,1,0:T(8,128)(2,1)S(1)} %get-tuple-element.401), channel_id=1, source_target_pairs={{0,4},{4,8},{8,12},{1,5},{5,9},{9,13},{2,6},{6,10},{10,14},{3,7},{... | collective-permute-start | bytes 516104 | tf_op jit(solution)/shard_map/ppermute | solution.py:15
  47.5 6.2 %collective-permute-start.3 = (bf16[14,3,16,128]{3,2,1,0:T(8,128)(2,1)S(1)}, bf16[14,3,16,128]{3,2,1,0:T(8,128)(2,1)}, u32[]{:S(2)}, u32[]{:S(2)}) collective-permute-start(bf16[14,3,16,128]{3,2,1,0:T(8,128)(2,1)S(1)} %get-tuple-element.402), channel_id=1, source_target_pairs={{4,0},{8,4},{12,8},{5,1},{9,5},{13,9},{6,2},{10,6},{14,10},{7,3},{... | collective-permute-start | bytes 516104 | tf_op jit(solution)/shard_map/ppermute | solution.py:18
  57.2 3.5 copy-start.13
  77.2 2.7 copy-start.2
  109.3 2.7 copy-start.2
  188.9 7.0 %copy-start.3 = (f32[14,22,16,128]{3,2,1,0:T(8,128)S(1)}, f32[14,22,16,128]{3,2,1,0:T(8,128)}, u32[]{:S(2)}) copy-start(f32[14,22,16,128]{3,2,1,0:T(8,128)} %get-tuple-element.223) | copy-start | bytes 7569412
  191.0 7.5 %collective-permute-start.8 = (bf16[3,22,16,128]{3,2,1,0:T(8,128)(2,1)S(1)}, bf16[3,22,16,128]{3,2,1,0:T(8,128)(2,1)S(1)}, u32[]{:S(2)}, u32[]{:S(2)}) collective-permute-start(bf16[3,22,16,128]{3,2,1,0:T(8,128)(2,1)S(1)} %get-tuple-element.399), channel_id=1, source_target_pairs={{0,16},{16,32},{32,48},{48,64},{64,80},{80,96},{96,112},{1,17},{17... | collective-permute-start | bytes 811016 | tf_op jit(solution)/shard_map/ppermute | solution.py:15
  194.6 11.3 %collective-permute-start.9 = (bf16[3,22,16,128]{3,2,1,0:T(8,128)(2,1)S(1)}, bf16[3,22,16,128]{3,2,1,0:T(8,128)(2,1)S(1)}, u32[]{:S(2)}, u32[]{:S(2)}) collective-permute-start(bf16[3,22,16,128]{3,2,1,0:T(8,128)(2,1)S(1)} %get-tuple-element.400), channel_id=1, source_target_pairs={{16,0},{32,16},{48,32},{64,48},{80,64},{96,80},{112,96},{17,1},{33... | collective-permute-start | bytes 811016 | tf_op jit(solution)/shard_map/ppermute | solution.py:18
  205.9 9.0 %copy-start.8 = (bf16[8,16,16,64]{3,2,1,0:T(8,128)(2,1)S(1)}, bf16[8,16,16,64]{3,2,1,0:T(8,128)(2,1)}, u32[]{:S(2)}) copy-start(bf16[8,16,16,64]{3,2,1,0:T(8,128)(2,1)} %get-tuple-element.222) | copy-start | bytes 786436
  206.8 10.1 %collective-permute-start.10 = (bf16[8,3,16,128]{3,2,1,0:T(8,128)(2,1)}, bf16[8,3,16,128]{3,2,1,0:T(8,128)(2,1)}, u32[]{:S(2)}, u32[]{:S(2)}) collective-permute-start(bf16[8,3,16,128]{3,2,1,0:T(8,128)(2,1)} %get-tuple-element.405), channel_id=1, source_target_pairs={{0,4},{4,8},{8,12},{1,5},{5,9},{9,13},{2,6},{6,10},{10,14},{3,7},{... | collective-permute-start | bytes 294920 | tf_op jit(solution)/shard_map/ppermute | solution.py:15
  213.6 6.3 %collective-permute-start.11 = (bf16[8,3,16,128]{3,2,1,0:T(8,128)(2,1)}, bf16[8,3,16,128]{3,2,1,0:T(8,128)(2,1)}, u32[]{:S(2)}, u32[]{:S(2)}) collective-permute-start(bf16[8,3,16,128]{3,2,1,0:T(8,128)(2,1)} %get-tuple-element.406), channel_id=1, source_target_pairs={{4,0},{8,4},{12,8},{5,1},{9,5},{13,9},{6,2},{10,6},{14,10},{7,3},{... | collective-permute-start | bytes 294920 | tf_op jit(solution)/shard_map/ppermute | solution.py:18
  216.9 9.6 %copy-start.9 = (bf16[2048,1,1,64]{0,3,2,1:T(8,128)(2,1)S(1)}, bf16[2048,1,1,64]{0,3,2,1:T(8,128)(2,1)}, u32[]{:S(2)}) copy-start(bf16[2048,1,1,64]{0,3,2,1:T(8,128)(2,1)} %copy.53) | copy-start | bytes 786436
  229.1 5.4 %copy-start.10 = (bf16[384,192]{0,1:T(8,128)(2,1)S(1)}, bf16[384,192]{0,1:T(8,128)(2,1)}, u32[]{:S(2)}) copy-start(bf16[384,192]{0,1:T(8,128)(2,1)} %param.16) | copy-start | bytes 442372
  230.3 182.4 %reduce-scatter.4.cloned.1.call-start = ((), (), s32[]{:S(2)}) async-start(), calls=%async_computation.2 | async-start | bytes 3932160
  (10 other events, 17.2 us)
Sparse Core Ops, SparseCore 0:
  230.5 102.9 all-reduce.1
Sparse Core Ops, SparseCore 1:
  279.2 42.6 reduce-scatter.3
where the time goes:
time: 432 us; the launch traced here: 430 us
  local copies, waits for them, and re-layouts  141 us (33%)
  blocking collectives  129 us (30%)
  matrix products  57 us (13%)
  other arithmetic  38.5 us (9%)
  starting transfers between devices  35 us (8%)
  between operations  15.9 us (4%)
  waiting for transfers between devices  13.2 us (3%)
    psum x1, blocking collectives, shards(): lax.psum(part_output.astype(jnp.bfloat16), ('gx', 'gy')).astype(jnp.float32)  129 us
    unnamed x34, local copies, waits for them, and re-layouts  60.2 us
    ppermute x6, starting transfers between devices, extended(): lax.ppermute(lax.slice_in_dim(block, block.shape[dim] - width, None, axis...  27.2 us
    dot_general x4, matrix products, attend_block(): jnp.einsum('qhe,khe->hqk', query_block, keys_block, preferred_element_typ...  23.3 us
    another operation x4, local copies, waits for them, and re-layouts, attend_block(): jnp.stack([key_gradient, value_gradient], axis=2)  13.1 us
    reshape x4, local copies, waits for them, and re-layouts, attend_block(): jnp.stack([key_gradient, value_gradient], axis=2)  12.6 us
    dynamic_update_slice x4, other arithmetic, attend_block(): lax.dynamic_update_slice_in_dim(pair_sums, previous + pair_gradient, firs...  10.7 us
    ppermute x6, waiting for transfers between devices, extended(): lax.ppermute(lax.slice_in_dim(block, 0, width, axis=dim), axis, backward)  10.7 us
  transfers between devices with their start and end apart: 14, of which 4 were waited for; matrix products, arithmetic and copies ran while one was open for 17% of the time, Pallas kernels for 0%

commit v1 on v0

--- a/solution.py
+++ b/solution.py
@@ -186,7 +186,7 @@
     )
     summed_input, summed_output = (
         lax.psum(part_input.astype(jnp.bfloat16), ("gx", "gy")).astype(jnp.float32),
-        lax.psum(part_output.astype(jnp.bfloat16), ("gx", "gy")).astype(jnp.float32),
+        lax.psum(lax.psum(part_output.astype(jnp.bfloat16), "gy"), "gx").astype(jnp.float32),
     )
     normaliser = (token_count * lax.axis_size("gx") * lax.axis_size("gy")) ** (-0.5)
     return (token_gradient, summed_input * normaliser, summed_output * normaliser)

time: 432 us -> 357 us (0.83)
  blocking collectives: 129 us -> 50.8 us
    psum x1 -> x2, blocking collectives: 129 us -> 50.8 us  [the longest x1 32.2 us: shards(): lax.psum(lax.psum(part_output.astype(jnp.bfloat16), 'gy'), 'gx')]
  transfers between devices with their start and end apart: 14 -> 14, of which waited for: 4 -> 4; matrix products, arithmetic and copies ran while one was open for 17% -> 21% of each run, Pallas kernels for 0% -> 0%
where the time goes in v1:
time: 357 us; the launch traced here: 352 us
  local copies, waits for them, and re-layouts  141 us (39%)
  matrix products  57 us (16%)
  blocking collectives  50.8 us (14%)
  other arithmetic  38.4 us (11%)
  starting transfers between devices  35 us (10%)
  between operations  15.9 us (4%)
  waiting for transfers between devices  13.3 us (4%)
    unnamed x34, local copies, waits for them, and re-layouts  60.3 us
    psum x1, blocking collectives, shards(): lax.psum(lax.psum(part_output.astype(jnp.bfloat16), 'gy'), 'gx')  32.2 us
    ppermute x6, starting transfers between devices, extended(): lax.ppermute(lax.slice_in_dim(block, block.shape[dim] - width, None, axis...  27.2 us
    dot_general x4, matrix products, attend_block(): jnp.einsum('qhe,khe->hqk', query_block, keys_block, preferred_element_typ...  23.3 us
    psum x1, blocking collectives, shards(): lax.psum(part_output.astype(jnp.bfloat16), 'gy')  18.6 us
    another operation x4, local copies, waits for them, and re-layouts, attend_block(): jnp.stack([key_gradient, value_gradient], axis=2)  13.2 us
    reshape x4, local copies, waits for them, and re-layouts, attend_block(): jnp.stack([key_gradient, value_gradient], axis=2)  12.6 us
    ppermute x6, waiting for transfers between devices, extended(): lax.ppermute(lax.slice_in_dim(block, 0, width, axis=dim), axis, backward)  10.7 us
  transfers between devices with their start and end apart: 14, of which 4 were waited for; matrix products, arithmetic and copies ran while one was open for 21% of the time, Pallas kernels for 0%

profile of v1, /device:TPU:0, one launch (start us, length us, event | category | flops | bytes accessed | tf_op | source)
XLA Modules:
  0.0 352.1 jit_solution(7356172773218308765)
XLA Ops:
  11.0 3.5 collective-permute-start.4
  24.8 5.8 %collective-permute-start = (bf16[3,16,16,128]{3,2,1,0:T(8,128)(2,1)}, bf16[3,16,16,128]{3,2,1,0:T(8,128)(2,1)}, u32[]{:S(2)}, u32[]{:S(2)}) collective-permute-start(bf16[3,16,16,128]{3,2,1,0:T(8,128)(2,1)} %slice.209), channel_id=1, source_target_pairs={{0,16},{16,32},{32,48},{48,64},{64,80},{80,96},{96,112},{1,17},{17... | collective-permute-start | bytes 589832 | tf_op jit(solution)/shard_map/ppermute | solution.py:15
  41.4 6.2 %collective-permute-start.2 = (bf16[14,3,16,128]{3,2,1,0:T(8,128)(2,1)S(1)}, bf16[14,3,16,128]{3,2,1,0:T(8,128)(2,1)S(1)}, u32[]{:S(2)}, u32[]{:S(2)}) collective-permute-start(bf16[14,3,16,128]{3,2,1,0:T(8,128)(2,1)S(1)} %get-tuple-element.401), channel_id=1, source_target_pairs={{0,4},{4,8},{8,12},{1,5},{5,9},{9,13},{2,6},{6,10},{10,14},{3,7},{... | collective-permute-start | bytes 516104 | tf_op jit(solution)/shard_map/ppermute | solution.py:15
  60.7 128.3 %while.23 = (s32[]{:T(128)}, bf16[8,16,16,64]{3,2,1,0:T(8,128)(2,1)}, f32[14,22,16,128]{3,2,1,0:T(8,128)}, bf16[8,16,16,64]{3,2,1,0:T(8,128)(2,1)}, bf16[14,22,1...) while((s32[]{:T(128)}, ...), condition=%wide.region_4.5_spmd.clone.clone, body=%wide.region_0.4_spmd.clone.clone.sunk | while | flops 1152845056 | bytes 82846784 | solution.py:152
  66.3 5.8 %fusion.85 = (f32[512]{0:T(512)S(1)}, f32[512,2816]{1,0:T(8,128)S(1)}) fusion(bf16[512,64]{1,0:T(8,128)(2,1)S(1)} %bitcast.150, bf16[2816,1,2,64]{3,0,2,1:T(8,128)(2,1)S(1)} %bitcast.143, pred[2816]{0:T(1024)(128)(4,1)S(1)} %gt.22, s32[2816]{0:T(1024)S(1)} %get-tuple-element.564, s32[512]{0:T(512)S(1)} %get-tuple-element.565, ...), kind=kOutput, calls=%fused_computation.123.clone.1 | convolution fusion | flops 214826496 | bytes 6667264 | tf_op jit(solution)/shard_map/while/body/eval_jaxpr/qhe,khe->hqk/dot_general | solution.py:100
  83.7 3.3 copy.74
  87.0 3.2 reshape.514
  98.4 5.8 %fusion.85 = (f32[512]{0:T(512)S(1)}, f32[512,2816]{1,0:T(8,128)S(1)}) fusion(bf16[512,64]{1,0:T(8,128)(2,1)S(1)} %bitcast.150, bf16[2816,1,2,64]{3,0,2,1:T(8,128)(2,1)S(1)} %bitcast.143, pred[2816]{0:T(1024)(128)(4,1)S(1)} %gt.22, s32[2816]{0:T(1024)S(1)} %get-tuple-element.564, s32[512]{0:T(512)S(1)} %get-tuple-element.565, ...), kind=kOutput, calls=%fused_computation.123.clone.1 | convolution fusion | flops 214826496 | bytes 6667264 | tf_op jit(solution)/shard_map/while/body/eval_jaxpr/qhe,khe->hqk/dot_general | solution.py:100
  115.7 3.3 copy.74
  119.0 3.2 reshape.514
  130.5 5.8 %fusion.85 = (f32[512]{0:T(512)S(1)}, f32[512,2816]{1,0:T(8,128)S(1)}) fusion(bf16[512,64]{1,0:T(8,128)(2,1)S(1)} %bitcast.150, bf16[2816,1,2,64]{3,0,2,1:T(8,128)(2,1)S(1)} %bitcast.143, pred[2816]{0:T(1024)(128)(4,1)S(1)} %gt.22, s32[2816]{0:T(1024)S(1)} %get-tuple-element.564, s32[512]{0:T(512)S(1)} %get-tuple-element.565, ...), kind=kOutput, calls=%fused_computation.123.clone.1 | convolution fusion | flops 214826496 | bytes 6667264 | tf_op jit(solution)/shard_map/while/body/eval_jaxpr/qhe,khe->hqk/dot_general | solution.py:100
  147.8 3.3 copy.74
  162.6 5.8 %fusion.85 = (f32[512]{0:T(512)S(1)}, f32[512,2816]{1,0:T(8,128)S(1)}) fusion(bf16[512,64]{1,0:T(8,128)(2,1)S(1)} %bitcast.150, bf16[2816,1,2,64]{3,0,2,1:T(8,128)(2,1)S(1)} %bitcast.143, pred[2816]{0:T(1024)(128)(4,1)S(1)} %gt.22, s32[2816]{0:T(1024)S(1)} %get-tuple-element.564, s32[512]{0:T(512)S(1)} %get-tuple-element.565, ...), kind=kOutput, calls=%fused_computation.123.clone.1 | convolution fusion | flops 214826496 | bytes 6667264 | tf_op jit(solution)/shard_map/while/body/eval_jaxpr/qhe,khe->hqk/dot_general | solution.py:100
  179.9 3.3 copy.74
  191.1 3.6 %collective-permute-start.8 = (bf16[3,22,16,128]{3,2,1,0:T(8,128)(2,1)S(1)}, bf16[3,22,16,128]{3,2,1,0:T(8,128)(2,1)S(1)}, u32[]{:S(2)}, u32[]{:S(2)}) collective-permute-start(bf16[3,22,16,128]{3,2,1,0:T(8,128)(2,1)S(1)} %get-tuple-element.399), channel_id=1, source_target_pairs={{0,16},{16,32},{32,48},{48,64},{64,80},{80,96},{96,112},{1,17},{17... | collective-permute-start | bytes 811016 | tf_op jit(solution)/shard_map/ppermute | solution.py:15
  198.6 7.3 %collective-permute-done.9 = bf16[3,22,16,128]{3,2,1,0:T(8,128)(2,1)S(1)} collective-permute-done((bf16[3,22,16,128]{3,2,1,0:T(8,128)(2,1)S(1)}, bf16[3,22,16,128]{3,2,1,0:T(8,128)(2,1)S(1)}, u32[]{:S(2)}, u32[]{:S(2)}) %collective-permute-start.9) | collective-permute-done | bytes 270368 | tf_op jit(solution)/shard_map/ppermute | solution.py:18
  207.0 6.8 %collective-permute-start.10 = (bf16[8,3,16,128]{3,2,1,0:T(8,128)(2,1)}, bf16[8,3,16,128]{3,2,1,0:T(8,128)(2,1)}, u32[]{:S(2)}, u32[]{:S(2)}) collective-permute-start(bf16[8,3,16,128]{3,2,1,0:T(8,128)(2,1)} %get-tuple-element.405), channel_id=1, source_target_pairs={{0,4},{4,8},{8,12},{1,5},{5,9},{9,13},{2,6},{6,10},{10,14},{3,7},{... | collective-permute-start | bytes 294920 | tf_op jit(solution)/shard_map/ppermute | solution.py:15
  230.5 4.1 %convert_element_type.112 = bf16[8,16,16,192]{3,2,1,0:T(8,128)(2,1)S(1)} reshape(bf16[2048,1,3,64]{3,2,0,1:T(4,128)(2,1)} %copy.55) | data formatting | bytes 1572864 | tf_op jit(solution)/shard_map/convert_element_type | solution.py:172
  237.0 20.4 %copy.58 = f32[8,16,16,384]{2,1,0,3:T(8,128)} copy(f32[8,16,16,384]{3,2,1,0:T(8,128)} %fusion.14) | data formatting | bytes 6291456
  257.4 21.8 %reshape.511 = f32[384,2048]{1,0:T(8,128)} reshape(f32[384,8,16,16]{3,2,1,0:T(8,128)} %bitcast.147) | data formatting | bytes 6291456
  282.0 18.6 %psum.22 = bf16[64,384]{1,0:T(8,128)(2,1)S(1)} all-reduce(bf16[64,384]{1,0:T(8,128)(2,1)S(1)} %fusion.9), channel_id=1, replica_groups=mesh['gx'=8,'gy'=4,'ha'=4] {'gy'}, use_global_device_ids=true, to_apply=%region_7.8 | all-reduce | flops 24576 | bytes 98304 | tf_op jit(solution)/shard_map/psum | solution.py:189
  300.6 32.2 %psum.23 = bf16[64,384]{1,0:T(8,128)(2,1)S(1)} all-reduce(bf16[64,384]{1,0:T(8,128)(2,1)S(1)} %psum.22), channel_id=1, replica_groups=mesh['gx'=8,'gy'=4,'ha'=4] {'gx'}, use_global_device_ids=true, to_apply=%region_8.9 | all-reduce | flops 24576 | bytes 98304 | tf_op jit(solution)/shard_map/psum | solution.py:189
  335.2 4.7 %reshape.512 = bf16[96,8,16,16]{3,2,1,0:T(8,128)(2,1)} reshape(f32[96,2048]{1,0:T(8,128)} %reduce-scatter.4.cloned.1.call-done) | data formatting | bytes 1179648
  339.8 4.8 %copy.59 = bf16[8,16,16,96]{3,2,1,0:T(8,128)(2,1)} copy(bf16[8,16,16,96]{2,1,0,3:T(8,128)(2,1)} %bitcast.154) | data formatting | bytes 786432
  (198 shorter events, 153.3 us)
Async XLA Ops:
  8.0 7.8 %copy-start = (bf16[8,16,16,384]{3,2,1,0:T(8,128)(2,1)S(1)}, bf16[8,16,16,384]{3,2,1,0:T(8,128)(2,1)}, u32[]{:S(2)}) copy-start(bf16[8,16,16,384]{3,2,1,0:T(8,128)(2,1)} %param.15) | copy-start | bytes 4718596
  8.0 325.5 %all-reduce.2.cloned.1.call-start = ((), (), s32[]{:S(2)}) async-start(), calls=%async_computation.1 | async-start | bytes 294912 | tf_op jit(solution)/shard_map/psum | solution.py:188
  10.3 5.4 %copy-start.11 = (bf16[8,16,16]{2,1,0:T(8,128)(2,1)}, bf16[8,16,16]{2,1,0:T(8,128)(2,1)S(1)}, u32[]{:S(2)}) copy-start(bf16[8,16,16]{2,1,0:T(8,128)(2,1)S(1)} %fusion.17) | copy-start | bytes 12292
  11.0 24.1 %collective-permute-start.4 = (bf16[3,16,16]{2,1,0:T(8,128)(2,1)}, bf16[3,16,16]{2,1,0:T(8,128)(2,1)S(1)}, u32[]{:S(2)}, u32[]{:S(2)}) collective-permute-start(bf16[3,16,16]{2,1,0:T(8,128)(2,1)} %get-tuple-element.409), channel_id=1, source_target_pairs={{0,16},{16,32},{32,48},{48,64},{64,80},{80,96},{96,112},{1,17},{17... | collective-permute-start | bytes 4616 | tf_op jit(solution)/shard_map/ppermute | solution.py:15
  14.5 20.6 %collective-permute-start.5 = (bf16[3,16,16]{2,1,0:T(8,128)(2,1)}, bf16[3,16,16]{2,1,0:T(8,128)(2,1)}, u32[]{:S(2)}, u32[]{:S(2)}) collective-permute-start(bf16[3,16,16]{2,1,0:T(8,128)(2,1)} %get-tuple-element.410), channel_id=1, source_target_pairs={{16,0},{32,16},{48,32},{64,48},{80,64},{96,80},{112,96},{17,1},{33... | collective-permute-start | bytes 4616 | tf_op jit(solution)/shard_map/ppermute | solution.py:18
  15.8 15.5 %copy-start.4 = (bf16[8,16,16,384]{3,2,1,0:T(8,128)(2,1)S(1)}, bf16[8,16,16,384]{3,2,1,0:T(8,128)(2,1)}, u32[]{:S(2)}) copy-start(bf16[8,16,16,384]{3,2,1,0:T(8,128)(2,1)} %param.19) | copy-start | bytes 4718596
  21.4 18.1 %collective-permute-start.1 = (bf16[3,16,16,128]{3,2,1,0:T(8,128)(2,1)}, bf16[3,16,16,128]{3,2,1,0:T(8,128)(2,1)}, u32[]{:S(2)}, u32[]{:S(2)}) collective-permute-start(bf16[3,16,16,128]{3,2,1,0:T(8,128)(2,1)} %slice.212), channel_id=1, source_target_pairs={{16,0},{32,16},{48,32},{64,48},{80,64},{96,80},{112,96},{17,1},{33... | collective-permute-start | bytes 589832 | tf_op jit(solution)/shard_map/ppermute | solution.py:18
  24.8 13.6 %collective-permute-start = (bf16[3,16,16,128]{3,2,1,0:T(8,128)(2,1)}, bf16[3,16,16,128]{3,2,1,0:T(8,128)(2,1)}, u32[]{:S(2)}, u32[]{:S(2)}) collective-permute-start(bf16[3,16,16,128]{3,2,1,0:T(8,128)(2,1)} %slice.209), channel_id=1, source_target_pairs={{0,16},{16,32},{32,48},{48,64},{64,80},{80,96},{96,112},{1,17},{17... | collective-permute-start | bytes 589832 | tf_op jit(solution)/shard_map/ppermute | solution.py:15
  35.8 16.2 %collective-permute-start.6 = (bf16[14,3,16]{2,1,0:T(4,128)(2,1)S(1)}, bf16[14,3,16]{2,1,0:T(4,128)(2,1)S(1)}, u32[]{:S(2)}, u32[]{:S(2)}) collective-permute-start(bf16[14,3,16]{2,1,0:T(4,128)(2,1)S(1)} %get-tuple-element.407), channel_id=1, source_target_pairs={{0,4},{4,8},{8,12},{1,5},{5,9},{9,13},{2,6},{6,10},{10,14},{3,7},{... | collective-permute-start | bytes 4040 | tf_op jit(solution)/shard_map/ppermute | solution.py:15
  37.1 14.9 %collective-permute-start.7 = (bf16[14,3,16]{2,1,0:T(4,128)(2,1)S(1)}, bf16[14,3,16]{2,1,0:T(4,128)(2,1)S(1)}, u32[]{:S(2)}, u32[]{:S(2)}) collective-permute-start(bf16[14,3,16]{2,1,0:T(4,128)(2,1)S(1)} %get-tuple-element.408), channel_id=1, source_target_pairs={{4,0},{8,4},{12,8},{5,1},{9,5},{13,9},{6,2},{10,6},{14,10},{7,3},{... | collective-permute-start | bytes 4040 | tf_op jit(solution)/shard_map/ppermute | solution.py:18
  41.4 12.0 %collective-permute-start.2 = (bf16[14,3,16,128]{3,2,1,0:T(8,128)(2,1)S(1)}, bf16[14,3,16,128]{3,2,1,0:T(8,128)(2,1)S(1)}, u32[]{:S(2)}, u32[]{:S(2)}) collective-permute-start(bf16[14,3,16,128]{3,2,1,0:T(8,128)(2,1)S(1)} %get-tuple-element.401), channel_id=1, source_target_pairs={{0,4},{4,8},{8,12},{1,5},{5,9},{9,13},{2,6},{6,10},{10,14},{3,7},{... | collective-permute-start | bytes 516104 | tf_op jit(solution)/shard_map/ppermute | solution.py:15
  47.6 6.2 %collective-permute-start.3 = (bf16[14,3,16,128]{3,2,1,0:T(8,128)(2,1)S(1)}, bf16[14,3,16,128]{3,2,1,0:T(8,128)(2,1)}, u32[]{:S(2)}, u32[]{:S(2)}) collective-permute-start(bf16[14,3,16,128]{3,2,1,0:T(8,128)(2,1)S(1)} %get-tuple-element.402), channel_id=1, source_target_pairs={{4,0},{8,4},{12,8},{5,1},{9,5},{13,9},{6,2},{10,6},{14,10},{7,3},{... | collective-permute-start | bytes 516104 | tf_op jit(solution)/shard_map/ppermute | solution.py:18
  57.3 3.5 copy-start.13
  77.3 2.7 copy-start.2
  109.3 2.7 copy-start.2
  189.0 7.0 %copy-start.3 = (f32[14,22,16,128]{3,2,1,0:T(8,128)S(1)}, f32[14,22,16,128]{3,2,1,0:T(8,128)}, u32[]{:S(2)}) copy-start(f32[14,22,16,128]{3,2,1,0:T(8,128)} %get-tuple-element.223) | copy-start | bytes 7569412
  191.1 7.5 %collective-permute-start.8 = (bf16[3,22,16,128]{3,2,1,0:T(8,128)(2,1)S(1)}, bf16[3,22,16,128]{3,2,1,0:T(8,128)(2,1)S(1)}, u32[]{:S(2)}, u32[]{:S(2)}) collective-permute-start(bf16[3,22,16,128]{3,2,1,0:T(8,128)(2,1)S(1)} %get-tuple-element.399), channel_id=1, source_target_pairs={{0,16},{16,32},{32,48},{48,64},{64,80},{80,96},{96,112},{1,17},{17... | collective-permute-start | bytes 811016 | tf_op jit(solution)/shard_map/ppermute | solution.py:15
  194.7 11.3 %collective-permute-start.9 = (bf16[3,22,16,128]{3,2,1,0:T(8,128)(2,1)S(1)}, bf16[3,22,16,128]{3,2,1,0:T(8,128)(2,1)S(1)}, u32[]{:S(2)}, u32[]{:S(2)}) collective-permute-start(bf16[3,22,16,128]{3,2,1,0:T(8,128)(2,1)S(1)} %get-tuple-element.400), channel_id=1, source_target_pairs={{16,0},{32,16},{48,32},{64,48},{80,64},{96,80},{112,96},{17,1},{33... | collective-permute-start | bytes 811016 | tf_op jit(solution)/shard_map/ppermute | solution.py:18
  206.0 9.0 %copy-start.8 = (bf16[8,16,16,64]{3,2,1,0:T(8,128)(2,1)S(1)}, bf16[8,16,16,64]{3,2,1,0:T(8,128)(2,1)}, u32[]{:S(2)}) copy-start(bf16[8,16,16,64]{3,2,1,0:T(8,128)(2,1)} %get-tuple-element.222) | copy-start | bytes 786436
  207.0 10.1 %collective-permute-start.10 = (bf16[8,3,16,128]{3,2,1,0:T(8,128)(2,1)}, bf16[8,3,16,128]{3,2,1,0:T(8,128)(2,1)}, u32[]{:S(2)}, u32[]{:S(2)}) collective-permute-start(bf16[8,3,16,128]{3,2,1,0:T(8,128)(2,1)} %get-tuple-element.405), channel_id=1, source_target_pairs={{0,4},{4,8},{8,12},{1,5},{5,9},{9,13},{2,6},{6,10},{10,14},{3,7},{... | collective-permute-start | bytes 294920 | tf_op jit(solution)/shard_map/ppermute | solution.py:15
  213.7 6.3 %collective-permute-start.11 = (bf16[8,3,16,128]{3,2,1,0:T(8,128)(2,1)}, bf16[8,3,16,128]{3,2,1,0:T(8,128)(2,1)}, u32[]{:S(2)}, u32[]{:S(2)}) collective-permute-start(bf16[8,3,16,128]{3,2,1,0:T(8,128)(2,1)} %get-tuple-element.406), channel_id=1, source_target_pairs={{4,0},{8,4},{12,8},{5,1},{9,5},{13,9},{6,2},{10,6},{14,10},{7,3},{... | collective-permute-start | bytes 294920 | tf_op jit(solution)/shard_map/ppermute | solution.py:18
  217.0 9.6 %copy-start.9 = (bf16[2048,1,1,64]{0,3,2,1:T(8,128)(2,1)S(1)}, bf16[2048,1,1,64]{0,3,2,1:T(8,128)(2,1)}, u32[]{:S(2)}) copy-start(bf16[2048,1,1,64]{0,3,2,1:T(8,128)(2,1)} %copy.53) | copy-start | bytes 786436
  229.2 5.4 %copy-start.10 = (bf16[384,192]{0,1:T(8,128)(2,1)S(1)}, bf16[384,192]{0,1:T(8,128)(2,1)}, u32[]{:S(2)}) copy-start(bf16[384,192]{0,1:T(8,128)(2,1)} %param.16) | copy-start | bytes 442372
  230.5 104.7 %reduce-scatter.4.cloned.1.call-start = ((), (), s32[]{:S(2)}) async-start(), calls=%async_computation.2 | async-start | bytes 3932160
  (10 other events, 17.3 us)
Sparse Core Ops, SparseCore 0:
  230.6 102.9 all-reduce.1
Sparse Core Ops, SparseCore 1:
  279.3 42.7 reduce-scatter.3
